TPU v7x, 512 devices: a whole 4x8x8 slice. The times are simulated.
512 devices in a mesh: curve: 64 (over z, x, core), split: 8 (over y).
Axes of the slice: x: 4, y: 8, z: 8, core: 2. Of those that a mesh axis runs over, the one named last changes fastest.
Arguments:
- rhs_load: float32 [8192, 512], P(('curve', 'split')), may hold values from -6 to 6
- stretch: float32 [3, 8192], P(None, ('curve', 'split')), may hold values from 0.5 to 4
- helm_shift: float32 [8192], P(('curve', 'split')), may hold values from 100 to 1000
- local_slot: int32 [8192, 512], P(('curve', 'split')), may hold values from 0 to 5487, as said below
- share_curve: int32 [64, 8, 4, 128], P('curve', 'split'), may hold values from 0 to 5488, as said below
- share_split: int32 [64, 8, 2, 128], P('curve', 'split'), may hold values from 0 to 5488, as said below
- coarse_slot: int32 [8, 8192], P(None, ('curve', 'split')), may hold values from 0 to 15
- x_vals: float32 [16, 8192], P(None, ('curve', 'split')), may hold values from -4 to 4
- x_cols: int32 [16, 8192], P(None, ('curve', 'split')), may hold values from 0 to 8191, as said below
- x_count: int32 [8192], P(('curve', 'split')), may hold values from 1 to 16, as said below
Outputs:
- solution: float32 [8192, 512], P(('curve', 'split'))
- residual: float32 [8192, 512], P(('curve', 'split'))
Inputs may be any that keep to these rules, and one draw needn't show every extreme that they name: `local_slot`: every slot 0 to 5487 of a device's node vector is named by one or more of its points. `share_curve`: each entry is a node slot of the device, or 5488 for an empty entry; the slots of one list are distinct; the list of device (c, s) for offset o and the partner's list for offset -o name shared nodes entry by entry and have equal numbers of filled entries, which come first; lists towards partitions that do not exist are empty; some list is full in every draw. `share_split`: as for share_curve, with partner (c, s + o) for the offsets -1 and 1. `x_cols`: entry 0 of row i is i; entries 1 to 7 lie within 32 of i; the later entries lie among the coarse unknowns of separator devices of a nested dissection of the device numbers, one level an entry. `x_count`: some rows use all 16 entries.
All inputs are finite; a program needn't handle non-finite values.
Results may differ from a plain program's by a relative error of at most 0.0009.
Values sent between devices are 32-bit elements; how exact they have to be, the bound alone decides.
No kernel may reach another device: no remote copies, remote signals or barrier semaphores. Data moves between devices by JAX's collectives and lax.ppermute only.
A program may use at most 64 MiB of HBM per device.

v0:
```python
import jax
import jax.numpy as jnp
import numpy as np
from jax import lax
from jax.sharding import PartitionSpec as P

ITERS = 4


def from_behind(block, axis, distance):
    devices = range(lax.axis_size(axis))
    route = [(i - distance, i) for i in devices if i - distance in devices]
    return lax.ppermute(block, axis, route)


def element_tables():
    poly_order = 7
    node_count = poly_order + 1
    gll_nodes = -np.cos(np.pi * np.arange(node_count) / poly_order)
    legendre = np.zeros((node_count, node_count))
    for sweep in range(60):
        legendre[:, 0] = 1.0
        legendre[:, 1] = gll_nodes
        for degree in range(2, node_count):
            legendre[:, degree] = (
                (2 * degree - 1) * gll_nodes * legendre[:, degree - 1]
                - (degree - 1) * legendre[:, degree - 2]
            ) / degree
        gll_nodes = gll_nodes - (
            gll_nodes * legendre[:, poly_order] - legendre[:, poly_order - 1]
        ) / (node_count * legendre[:, poly_order])
    for degree in range(2, node_count):
        legendre[:, degree] = (
            (2 * degree - 1) * gll_nodes * legendre[:, degree - 1]
            - (degree - 1) * legendre[:, degree - 2]
        ) / degree
    top_poly = legendre[:, poly_order]
    quad_weights = 2.0 / (poly_order * node_count * top_poly * top_poly)
    deriv_matrix = np.zeros((node_count, node_count))
    for row_index in range(node_count):
        for col_index in range(node_count):
            if row_index != col_index:
                deriv_matrix[row_index, col_index] = top_poly[row_index] / (
                    top_poly[col_index] * (gll_nodes[row_index] - gll_nodes[col_index])
                )
    deriv_matrix[0, 0] = -poly_order * node_count / 4.0
    deriv_matrix[poly_order, poly_order] = poly_order * node_count / 4.0
    identity = np.eye(node_count)
    mass_diag = (
        quad_weights[:, None, None] * quad_weights[None, :, None] * quad_weights[None, None, :]
    ).reshape(-1)
    stiff_list = []
    for deriv_kron in (
        np.kron(np.kron(deriv_matrix, identity), identity),
        np.kron(np.kron(identity, deriv_matrix), identity),
        np.kron(identity, np.kron(identity, deriv_matrix)),
    ):
        stiff_list.append(deriv_kron.T @ (mass_diag[:, None] * deriv_kron))
    stiffness = np.concatenate(stiff_list, axis=1)
    diag_index = np.arange(stiff_list[0].shape[0])
    stiff_diag = np.stack([block[diag_index, diag_index] for block in stiff_list])
    hat_values = np.stack([(1.0 - gll_nodes) / 2.0, (1.0 + gll_nodes) / 2.0])
    coarse_table = (
        hat_values[:, None, None, :, None, None]
        * hat_values[None, :, None, None, :, None]
        * hat_values[None, None, :, None, None, :]
    ).reshape(8, -1)
    return (mass_diag, stiffness, stiff_diag, coarse_table)


def local_operator(element_field, stiffness, mass_diag, stretch, helm_shift):
    products = jnp.dot(
        element_field,
        stiffness,
        precision=lax.Precision.HIGHEST,
        preferred_element_type=jnp.float32,
    )
    point_count = element_field.shape[1]
    result = stretch[0][:, None] * products[:, :point_count]
    result = result + stretch[1][:, None] * products[:, point_count : 2 * point_count]
    result = result + stretch[2][:, None] * products[:, 2 * point_count :]
    return result + helm_shift[:, None] * mass_diag[None, :] * element_field


def assemble(fields, point_slots, curve_lists, split_lists, node_count):
    batch_count = fields.shape[0]
    flattened = fields.reshape(batch_count, -1)
    node_sums = jax.vmap(
        lambda values: jax.ops.segment_sum(values, point_slots, num_segments=node_count + 1)
    )(flattened)
    assembled = node_sums
    for list_index, offset in enumerate((-1, 1)):
        outgoing = node_sums[:, split_lists[1 - list_index]]
        incoming = from_behind(outgoing, "split", -offset)
        assembled = assembled.at[:, split_lists[list_index]].add(incoming)
    reach = curve_lists.shape[0] // 2
    curve_offsets = list(range(-reach, 0)) + list(range(1, reach + 1))
    for list_index, offset in enumerate(curve_offsets):
        outgoing = node_sums[:, curve_lists[2 * reach - 1 - list_index]]
        incoming = from_behind(outgoing, "curve", -offset)
        assembled = assembled.at[:, curve_lists[list_index]].add(incoming)
    return assembled[:, point_slots].reshape(fields.shape)


def local(
    rhs_load,
    stretch,
    helm_shift,
    local_slot,
    share_curve,
    share_split,
    coarse_slot,
    x_vals,
    x_cols,
    x_count,
):
    mass_np, stiff_np, sdiag_np, coarse_np = element_tables()
    mass_diag = jnp.asarray(mass_np, dtype=jnp.float32)
    stiffness = jnp.asarray(stiff_np, dtype=jnp.float32)
    stiff_diag = jnp.asarray(sdiag_np, dtype=jnp.float32)
    coarse_table = jnp.asarray(coarse_np, dtype=jnp.float32)
    element_count = rhs_load.shape[0]
    node_count = 343 * element_count
    point_slots = local_slot.reshape(-1)
    curve_lists = share_curve.reshape(share_curve.shape[2], share_curve.shape[3])
    split_lists = share_split.reshape(share_split.shape[2], share_split.shape[3])
    coarse_rows = x_vals.shape[1]
    total_coarse = coarse_rows * lax.axis_size("curve") * lax.axis_size("split")
    diag_local = (
        stretch[0][:, None] * stiff_diag[0][None, :] + stretch[1][:, None] * stiff_diag[1][None, :]
    )
    diag_local = (
        diag_local
        + stretch[2][:, None] * stiff_diag[2][None, :]
        + helm_shift[:, None] * mass_diag[None, :]
    )
    setup = assemble(
        jnp.stack([jnp.ones_like(rhs_load), diag_local, rhs_load]),
        point_slots,
        curve_lists,
        split_lists,
        node_count,
    )
    multiplicity = setup[0]
    diag_a = setup[1]
    right = setup[2]
    live_entry = jnp.arange(x_vals.shape[0])[:, None] < x_count[None, :]
    factor = jnp.where(live_entry, x_vals, jnp.zeros_like(x_vals))

    def global_dot(left_field, right_field):
        return lax.psum(jnp.sum(left_field * right_field / multiplicity), ("curve", "split"))

    def coarse_partial(scaled):
        restricted = lax.dot_general(
            coarse_table,
            scaled,
            (((1,), (1,)), ((), ())),
            precision=lax.Precision.HIGHEST,
            preferred_element_type=jnp.float32,
        )
        loads = jax.ops.segment_sum(
            restricted.reshape(-1), coarse_slot.reshape(-1), num_segments=coarse_rows
        )
        return jax.ops.segment_sum(
            (factor * loads[None, :]).reshape(-1), x_cols.reshape(-1), num_segments=total_coarse
        )

    def coarse_correction(coarse_image):
        coarse_values = jnp.sum(factor * coarse_image[x_cols], axis=0)
        vertex_values = coarse_values[coarse_slot]
        return lax.dot_general(
            vertex_values,
            coarse_table,
            (((0,), (0,)), ((), ())),
            precision=lax.Precision.HIGHEST,
            preferred_element_type=jnp.float32,
        )

    def precondition(residual_field):
        scaled = residual_field / multiplicity
        partial_image = coarse_partial(scaled)
        jacobi_part = residual_field / diag_a
        coarse_image = lax.psum(partial_image, ("curve", "split"))
        precond_field = jacobi_part + coarse_correction(coarse_image)
        precond_norm = global_dot(residual_field, precond_field)
        return (precond_field, precond_norm)

    solution = jnp.zeros_like(rhs_load)
    residual = right
    precond, rz_value = precondition(residual)
    direction = precond
    for iteration in range(ITERS):
        image = assemble(
            local_operator(direction, stiffness, mass_diag, stretch, helm_shift)[None],
            point_slots,
            curve_lists,
            split_lists,
            node_count,
        )[0]
        step_size = rz_value / global_dot(direction, image)
        solution = solution + step_size * direction
        residual = residual - step_size * image
        if iteration < ITERS - 1:
            precond, rz_next = precondition(residual)
            direction = precond + rz_next / rz_value * direction
            rz_value = rz_next
    return (solution, residual)


def solution(mesh):
    in_specs = (
        P(("curve", "split"), None),
        P(None, ("curve", "split")),
        P(("curve", "split")),
        P(("curve", "split"), None),
        P("curve", "split", None, None),
        P("curve", "split", None, None),
        P(None, ("curve", "split")),
        P(None, ("curve", "split")),
        P(None, ("curve", "split")),
        P(("curve", "split")),
    )
    out_specs = (P(("curve", "split"), None), P(("curve", "split"), None))
    return jax.shard_map(local, mesh=mesh, in_specs=in_specs, out_specs=out_specs, check_vma=False)
```

profile of v0, /device:TPU:27, one launch (start us, length us, event | category | flops | bytes accessed | tf_op | source)
XLA Modules:
  0.0 1746.6 jit_solution(16968491514519512765)
XLA Ops:
  6.5 2.6 copy.18
  9.2 45.0 %scatter_custom_fusion = f32[3,5489]{0,1:T(8,128)S(1)} fusion(s32[8192]{0:T(1024)S(1)} %bitcast.195, f32[8192,3]{1,0:T(8,128)} %copy.18, f32[]{:T(128)} %constant.10.clone.1), kind=kCustom, calls=%fused_computation.89 | custom fusion | flops 24576 | bytes 66380 | tf_op jit(solution)/shard_map/vmap()/scatter-add | solution.py:89
  55.4 4.4 collective-permute-start
  60.5 1.9 collective-permute-start.1
  63.7 3.1 collective-permute-start.2
  67.4 3.9 collective-permute-start.3
  72.6 1.9 collective-permute-start.4
  76.1 2.5 collective-permute-start.5
  78.8 2.3 scatter_custom_fusion.1
  81.0 2.4 scatter_custom_fusion.2
  83.5 2.3 scatter_custom_fusion.3
  85.7 2.3 scatter_custom_fusion.4
  88.0 2.3 scatter_custom_fusion.5
  90.4 2.7 scatter_custom_fusion.6
  93.1 27.7 %gather_fusion.6 = f32[8192,3]{1,0:T(8,128)} fusion(f32[3,5489]{0,1:T(8,128)S(1)} %scatter_custom_fusion.6, s32[8192]{0:T(1024)S(1)} %broadcast_clamp_fusion), kind=kCustom, calls=%fused_computation.6 | custom fusion | bytes 229376 | tf_op jit(solution)/shard_map/gather | solution.py:102
  120.8 10.2 slice_reduce_fusion.1
  132.8 2.3 scatter_custom_fusion.8
  135.2 106.3 %psum.84 = f32[8192]{0:T(1024)S(1)} all-reduce(f32[8192]{0:T(1024)S(1)} %scatter_custom_fusion.8), channel_id=1, replica_groups=mesh['curve'=64,'split'=8] {'curve','split'}, use_global_device_ids=true, to_apply=%region_9.10 | all-reduce | flops 8192 | bytes 65536 | tf_op jit(solution)/shard_map/psum | solution.py:183
  246.8 43.4 %scatter_custom_fusion.9 = f32[5489]{0:T(1024)S(1)} fusion(s32[8192]{0:T(1024)S(1)} %bitcast.196, f32[8192]{0:T(1024)S(1)} %bitcast.201, f32[]{:T(128)} %constant.10.clone.1), kind=kCustom, calls=%fused_computation.198 | custom fusion | flops 8192 | bytes 21960 | tf_op jit(solution)/shard_map/vmap()/scatter-add | solution.py:89
  295.3 2.4 collective-permute-start.6
  300.2 2.9 collective-permute-start.7
  303.1 1.9 collective-permute-start.8
  305.1 4.2 collective-permute-start.9
  309.3 1.9 collective-permute-start.10
  311.2 2.2 collective-permute-start.11
  321.4 45.5 %gather_fusion.15 = f32[8192]{0:T(1024)S(1)} fusion(f32[5489]{0:T(1024)S(1)} %scatter_fusion.5, s32[8192]{0:T(1024)S(1)} %broadcast_clamp_fusion), kind=kCustom, calls=%fused_computation.15 | custom fusion | bytes 98304 | tf_op jit(solution)/shard_map/gather | solution.py:102
  367.6 100.7 %all-reduce = (f32[]{:T(128)}, f32[]{:T(128)}) all-reduce(f32[]{:T(128)} %get-tuple-element.6, f32[]{:T(128)} %get-tuple-element.5), channel_id=1, replica_groups=mesh['curve'=64,'split'=8] {'curve','split'}, use_global_device_ids=true, to_apply=%region_12.13 | all-reduce | flops 2 | bytes 16 | tf_op jit(solution)/shard_map/psum | solution.py:151
  471.6 2.5 scatter_custom_fusion.17
  474.1 94.6 %psum.87 = f32[8192]{0:T(1024)S(1)} all-reduce(f32[8192]{0:T(1024)S(1)} %scatter_custom_fusion.17), channel_id=1, replica_groups=mesh['curve'=64,'split'=8] {'curve','split'}, use_global_device_ids=true, to_apply=%region_24.25 | all-reduce | flops 8192 | bytes 65536 | tf_op jit(solution)/shard_map/psum | solution.py:183
  572.7 96.4 %psum.88 = f32[]{:T(128)} all-reduce(f32[]{:T(128)} %get-tuple-element.18), channel_id=1, replica_groups=mesh['curve'=64,'split'=8] {'curve','split'}, use_global_device_ids=true, to_apply=%region_27.28 | all-reduce | flops 1 | bytes 8 | tf_op jit(solution)/shard_map/psum | solution.py:151
  672.1 43.2 %scatter_custom_fusion.18 = f32[5489]{0:T(1024)S(1)} fusion(s32[8192]{0:T(1024)S(1)} %bitcast.197, f32[8192]{0:T(1024)S(1)} %bitcast.202, f32[]{:T(128)} %constant.10.clone.1), kind=kCustom, calls=%fused_computation.196 | custom fusion | flops 8192 | bytes 21960 | tf_op jit(solution)/shard_map/vmap()/scatter-add | solution.py:89
  720.4 2.2 collective-permute-start.12
  725.2 3.1 collective-permute-start.13
  728.3 1.9 collective-permute-start.14
  730.2 3.7 collective-permute-start.15
  734.0 1.9 collective-permute-start.16
  735.9 2.2 collective-permute-start.17
  746.1 45.5 %gather_fusion.24 = f32[8192]{0:T(1024)S(1)} fusion(f32[5489]{0:T(1024)S(1)} %scatter_fusion.11, s32[8192]{0:T(1024)S(1)} %broadcast_clamp_fusion), kind=kCustom, calls=%fused_computation.24 | custom fusion | bytes 98304 | tf_op jit(solution)/shard_map/gather | solution.py:102
  792.3 101.2 %psum.89 = f32[]{:T(128)} all-reduce(f32[]{:T(128)} %fusion.33), channel_id=1, replica_groups=mesh['curve'=64,'split'=8] {'curve','split'}, use_global_device_ids=true, to_apply=%region_36.37 | all-reduce | flops 1 | bytes 8 | tf_op jit(solution)/shard_map/psum | solution.py:151
  895.1 2.0 scatter_custom_fusion.25
  897.1 2.5 scatter_custom_fusion.26
  899.6 94.6 %psum.90 = f32[8192]{0:T(1024)S(1)} all-reduce(f32[8192]{0:T(1024)S(1)} %scatter_custom_fusion.26), channel_id=1, replica_groups=mesh['curve'=64,'split'=8] {'curve','split'}, use_global_device_ids=true, to_apply=%region_39.40 | all-reduce | flops 8192 | bytes 65536 | tf_op jit(solution)/shard_map/psum | solution.py:183
  998.2 96.3 %psum.91 = f32[]{:T(128)} all-reduce(f32[]{:T(128)} %get-tuple-element.20), channel_id=1, replica_groups=mesh['curve'=64,'split'=8] {'curve','split'}, use_global_device_ids=true, to_apply=%region_42.43 | all-reduce | flops 1 | bytes 8 | tf_op jit(solution)/shard_map/psum | solution.py:151
  1097.6 43.2 %scatter_custom_fusion.27 = f32[5489]{0:T(1024)S(1)} fusion(s32[8192]{0:T(1024)S(1)} %bitcast.198, f32[8192]{0:T(1024)S(1)} %bitcast.203, f32[]{:T(128)} %constant.10.clone.1), kind=kCustom, calls=%fused_computation.194 | custom fusion | flops 8192 | bytes 21960 | tf_op jit(solution)/shard_map/vmap()/scatter-add | solution.py:89
  1145.9 2.2 collective-permute-start.18
  1150.6 3.1 collective-permute-start.19
  1153.7 1.9 collective-permute-start.20
  1155.7 3.6 collective-permute-start.21
  1159.3 1.9 collective-permute-start.22
  1161.3 2.2 collective-permute-start.23
  1171.6 45.5 %gather_fusion.33 = f32[8192]{0:T(1024)S(1)} fusion(f32[5489]{0:T(1024)S(1)} %scatter_fusion.17, s32[8192]{0:T(1024)S(1)} %broadcast_clamp_fusion), kind=kCustom, calls=%fused_computation.33 | custom fusion | bytes 98304 | tf_op jit(solution)/shard_map/gather | solution.py:102
  1217.8 101.1 %psum.92 = f32[]{:T(128)} all-reduce(f32[]{:T(128)} %fusion.35), channel_id=1, replica_groups=mesh['curve'=64,'split'=8] {'curve','split'}, use_global_device_ids=true, to_apply=%region_51.52 | all-reduce | flops 1 | bytes 8 | tf_op jit(solution)/shard_map/psum | solution.py:151
  1322.1 2.5 scatter_custom_fusion.35
  1324.6 94.6 %psum.93 = f32[8192]{0:T(1024)S(1)} all-reduce(f32[8192]{0:T(1024)S(1)} %scatter_custom_fusion.35), channel_id=1, replica_groups=mesh['curve'=64,'split'=8] {'curve','split'}, use_global_device_ids=true, to_apply=%region_54.55 | all-reduce | flops 8192 | bytes 65536 | tf_op jit(solution)/shard_map/psum | solution.py:183
  1423.2 96.2 %psum.94 = f32[]{:T(128)} all-reduce(f32[]{:T(128)} %get-tuple-element.22), channel_id=1, replica_groups=mesh['curve'=64,'split'=8] {'curve','split'}, use_global_device_ids=true, to_apply=%region_57.58 | all-reduce | flops 1 | bytes 8 | tf_op jit(solution)/shard_map/psum | solution.py:151
  1522.4 43.2 %scatter_custom_fusion.36 = f32[5489]{0:T(1024)S(1)} fusion(s32[8192]{0:T(1024)S(1)} %bitcast.199, f32[8192]{0:T(1024)S(1)} %bitcast.200, f32[]{:T(128)} %constant.10.clone.1), kind=kCustom, calls=%fused_computation.192 | custom fusion | flops 8192 | bytes 21960 | tf_op jit(solution)/shard_map/vmap()/scatter-add | solution.py:89
  1570.8 2.2 collective-permute-start.24
  1575.5 3.1 collective-permute-start.25
  1578.6 1.9 collective-permute-start.26
  1580.5 3.7 collective-permute-start.27
  1584.3 2.1 collective-permute-start.28
  1586.4 2.2 collective-permute-start.29
  1596.6 45.5 %gather_fusion.42 = f32[8192]{0:T(1024)S(1)} fusion(f32[5489]{0:T(1024)S(1)} %scatter_fusion.23, s32[8192]{0:T(1024)S(1)} %broadcast_clamp_fusion), kind=kCustom, calls=%fused_computation.42 | custom fusion | bytes 98304 | tf_op jit(solution)/shard_map/gather | solution.py:102
  1642.8 101.1 %psum.95 = f32[]{:T(128)} all-reduce(f32[]{:T(128)} %fusion.37), channel_id=1, replica_groups=mesh['curve'=64,'split'=8] {'curve','split'}, use_global_device_ids=true, to_apply=%region_66.67 | all-reduce | flops 1 | bytes 8 | tf_op jit(solution)/shard_map/psum | solution.py:151
  (249 shorter events, 106.5 us)
Async XLA Ops:
  1.4 1096.0 %copy-start.6 = (f32[16]{0:T(128)}, f32[16]{0:T(128)S(1)}, u32[]{:S(2)}) copy-start(f32[16]{0:T(128)S(1)} %get-tuple-element.13) | copy-start | bytes 196
  1.4 1096.0 %copy-start.8 = (f32[16]{0:T(128)}, f32[16]{0:T(128)S(1)}, u32[]{:S(2)}) copy-start(f32[16]{0:T(128)S(1)} %get-tuple-element.14) | copy-start | bytes 196
  1.4 1096.0 %copy-start.10 = (f32[16]{0:T(128)}, f32[16]{0:T(128)S(1)}, u32[]{:S(2)}) copy-start(f32[16]{0:T(128)S(1)} %get-tuple-element.15) | copy-start | bytes 196
  1.5 7.6 copy-start.2
  1.6 7.5 copy-start.25
  6.4 56.0 %copy-start.23 = (s32[1,1,4,128]{3,2,1,0:T(4,128)S(1)}, s32[1,1,4,128]{3,2,1,0:T(4,128)}, u32[]{:S(2)}) copy-start(s32[1,1,4,128]{3,2,1,0:T(4,128)} %param.18) | copy-start | bytes 6148
  6.4 68.2 %copy-start.5 = (s32[16,16]{1,0:T(8,128)S(1)}, s32[16,16]{1,0:T(8,128)}, u32[]{:S(2)}) copy-start(s32[16,16]{1,0:T(8,128)} %param.22) | copy-start | bytes 3076
  6.5 68.3 %copy-start.12 = (s32[8,16]{1,0:T(8,128)S(1)}, s32[8,16]{1,0:T(8,128)}, u32[]{:S(2)}) copy-start(s32[8,16]{1,0:T(8,128)} %param.20) | copy-start | bytes 1540
  9.1 65.6 %copy-start.17 = (s32[1024]{0:T(1024)}, s32[1024]{0:T(1024)S(1)}, u32[]{:S(2)}) copy-start(s32[1024]{0:T(1024)S(1)} %get-tuple-element.26) | copy-start | bytes 12292
  9.1 81.2 %copy-start.18 = (s32[1024]{0:T(1024)}, s32[1024]{0:T(1024)S(1)}, u32[]{:S(2)}) copy-start(s32[1024]{0:T(1024)S(1)} %get-tuple-element.27) | copy-start | bytes 12292
  55.4 20.7 %collective-permute-start = (f32[3,128]{0,1:T(8,128)}, f32[3,128]{0,1:T(8,128)S(1)}, u32[]{:S(2)}, u32[]{:S(2)}) collective-permute-start(f32[3,128]{0,1:T(8,128)} %bitcast.8), channel_id=1, source_target_pairs={{0,1},{1,2},{2,3},{3,4},{4,5},{5,6},{6,7},{8,9},{9,10},{10,11},{11... | collective-permute-start | bytes 4616 | tf_op jit(solution)/shard_map/ppermute | solution.py:13
  60.5 20.6 %collective-permute-start.1 = (f32[3,128]{0,1:T(8,128)S(1)}, f32[3,128]{0,1:T(8,128)S(1)}, u32[]{:S(2)}, u32[]{:S(2)}) collective-permute-start(f32[3,128]{0,1:T(8,128)S(1)} %bitcast.252), channel_id=1, source_target_pairs={{1,0},{2,1},{3,2},{4,3},{5,4},{6,5},{7,6},{9,8},{10,9},{11,10},{12... | collective-permute-start | bytes 4616 | tf_op jit(solution)/shard_map/ppermute | solution.py:13
  62.4 21.0 %copy-start.19 = (s32[1024]{0:T(1024)}, s32[1024]{0:T(1024)S(1)}, u32[]{:S(2)}) copy-start(s32[1024]{0:T(1024)S(1)} %get-tuple-element.30) | copy-start | bytes 12292
  62.4 21.0 %copy-start.20 = (s32[1024]{0:T(1024)}, s32[1024]{0:T(1024)S(1)}, u32[]{:S(2)}) copy-start(s32[1024]{0:T(1024)S(1)} %get-tuple-element.31) | copy-start | bytes 12292
  63.7 19.8 %collective-permute-start.2 = (f32[3,128]{0,1:T(8,128)}, f32[3,128]{0,1:T(8,128)S(1)}, u32[]{:S(2)}, u32[]{:S(2)}) collective-permute-start(f32[3,128]{0,1:T(8,128)} %bitcast.16), channel_id=1, source_target_pairs={{0,16},{8,24},{16,32},{24,40},{32,48},{40,56},{48,64},{56,72},{64,... | collective-permute-start | bytes 4616 | tf_op jit(solution)/shard_map/ppermute | solution.py:13
  67.4 18.3 %collective-permute-start.3 = (f32[3,128]{0,1:T(8,128)S(1)}, f32[3,128]{0,1:T(8,128)S(1)}, u32[]{:S(2)}, u32[]{:S(2)}) collective-permute-start(f32[3,128]{0,1:T(8,128)S(1)} %bitcast.253), channel_id=1, source_target_pairs={{0,8},{8,16},{16,24},{24,32},{32,40},{40,48},{48,56},{56,64},{64,7... | collective-permute-start | bytes 4616 | tf_op jit(solution)/shard_map/ppermute | solution.py:13
  71.4 3.3 copy-start.22
  71.4 12.0 copy-start.21
  72.6 15.4 collective-permute-start.4
  76.1 14.2 collective-permute-start.5
  78.7 52.6 %copy-start.26 = (s32[128]{0:T(128)}, s32[128]{0:T(128)S(1)}, u32[]{:S(2)}) copy-start(s32[128]{0:T(128)S(1)} %reshape.851) | copy-start | bytes 1540
  78.8 54.1 %copy-start.24 = (s32[256]{0:T(256)}, s32[256]{0:T(256)S(1)}, u32[]{:S(2)}) copy-start(s32[256]{0:T(256)S(1)} %reshape.859) | copy-start | bytes 3076
  120.8 10.2 copy-start.13
  120.8 11.9 copy-start.1
  120.8 11.9 copy-start.4
  243.2 1.9 copy-start
  243.3 3.4 copy-start.3
  243.3 3.4 copy-start.15
  295.3 15.9 collective-permute-start.6
  300.2 14.6 collective-permute-start.7
  303.1 13.0 collective-permute-start.8
  305.1 12.4 collective-permute-start.9
  309.3 9.5 collective-permute-start.10
  311.2 8.9 collective-permute-start.11
  720.4 15.5 collective-permute-start.12
  725.2 14.3 collective-permute-start.13
  728.3 12.5 collective-permute-start.14
  730.2 11.9 collective-permute-start.15
  734.0 9.5 collective-permute-start.16
  735.9 8.9 collective-permute-start.17
  1145.9 15.4 collective-permute-start.18
  1150.6 14.2 collective-permute-start.19
  1153.7 12.5 collective-permute-start.20
  1155.7 11.8 collective-permute-start.21
  1159.3 9.5 collective-permute-start.22
  1161.3 9.0 collective-permute-start.23
  1171.6 148.6 %copy-start.14 = (f32[8,512]{1,0:T(8,128)S(1)}, f32[8,512]{1,0:T(8,128)}, u32[]{:S(2)}) copy-start(f32[8,512]{1,0:T(8,128)} %constant.4.clone) | copy-start | bytes 49156
  1422.2 100.1 %copy-start.7 = (f32[16]{0:T(128)S(1)}, f32[16]{0:T(128)}, u32[]{:S(2)}) copy-start(f32[16]{0:T(128)} %copy-done.6) | copy-start | bytes 196
  1422.2 100.1 %copy-start.9 = (f32[16]{0:T(128)S(1)}, f32[16]{0:T(128)}, u32[]{:S(2)}) copy-start(f32[16]{0:T(128)} %copy-done.8) | copy-start | bytes 196
  1422.2 100.1 %copy-start.11 = (f32[16]{0:T(128)S(1)}, f32[16]{0:T(128)}, u32[]{:S(2)}) copy-start(f32[16]{0:T(128)} %copy-done.10) | copy-start | bytes 196
  1422.3 100.1 %copy-start.16 = (f32[16]{0:T(128)S(1)}, f32[16]{0:T(128)}, u32[]{:S(2)}) copy-start(f32[16]{0:T(128)} %param.16) | copy-start | bytes 196
  1570.8 15.7 collective-permute-start.24
  1575.5 14.5 collective-permute-start.25
  1578.6 12.8 collective-permute-start.26
  1580.5 12.1 collective-permute-start.27
  1584.3 9.7 collective-permute-start.28
  1586.4 8.9 collective-permute-start.29
where the time goes:
time: 1760 us; the launch traced here: 1750 us
  blocking collectives  1080 us (61%)
  other arithmetic  285 us (16%)
  local copies, waits for them, and re-layouts  279 us (16%)
  starting transfers between devices  78.7 us (4%)
    psum x7, blocking collectives, global_dot(): lax.psum(jnp.sum(left_field * right_field / multiplicity), ('curve', 'spl...  693 us
    psum x4, blocking collectives, precondition(): coarse_image = lax.psum(partial_image, ('curve', 'split'))  390 us
    scatter-add x5, other arithmetic, assemble(): jax.ops.segment_sum(values, point_slots, num_segments=node_count + 1)  218 us
    gather x5, local copies, waits for them, and re-layouts, assemble(): return assembled[:, point_slots].reshape(fields.shape)  210 us
    ppermute x30, starting transfers between devices, from_behind(): return lax.ppermute(block, axis, route)  78.7 us
  transfers between devices with their start and end apart: 30, of which 0 were waited for; matrix products, arithmetic and copies ran while one was open for 3% of the time, Pallas kernels for 0%

commit v1 on v0

--- a/solution.py
+++ b/solution.py
@@ -180,7 +180,8 @@
         scaled = residual_field / multiplicity
         partial_image = coarse_partial(scaled)
         jacobi_part = residual_field / diag_a
-        coarse_image = lax.psum(partial_image, ("curve", "split"))
+        shards = lax.all_gather(partial_image, ("curve", "split"), axis=0, tiled=False)
+        coarse_image = shards.sum(axis=0)
         precond_field = jacobi_part + coarse_correction(coarse_image)
         precond_norm = global_dot(residual_field, precond_field)
         return (precond_field, precond_norm)

time: 1760 us -> 2020 us (1.15)
  waiting for transfers between devices: 0.08 us -> 533 us
  blocking collectives: 1080 us -> 692 us
  local copies, waits for them, and re-layouts: 279 us -> 352 us
  other arithmetic: 285 us -> 314 us
    all_gather x0 -> x4, waiting for transfers between devices: none -> 533 us  [precondition(): lax.all_gather(partial_image, ('curve', 'split'), axis=0, tiled=False)]
    psum x4 -> x0, blocking collectives: 390 us -> none  [precondition(): coarse_image = lax.psum(partial_image, ('curve', 'split'))]
    all_gather x0 -> x4, local copies, waits for them, and re-layouts: none -> 72.9 us  [precondition(): lax.all_gather(partial_image, ('curve', 'split'), axis=0, tiled=False)]
    reduce_sum x0 -> x4, other arithmetic: none -> 26.2 us  [precondition(): coarse_image = shards.sum(axis=0)]
  transfers between devices with their start and end apart: 30 -> 34, of which waited for: 0 -> 4; matrix products, arithmetic and copies ran while one was open for 3% -> 3% of each run, Pallas kernels for 0% -> 0%
where the time goes in v1:
time: 2020 us; the launch traced here: 2010 us
  blocking collectives  692 us (34%)
  waiting for transfers between devices  533 us (26%)
  local copies, waits for them, and re-layouts  352 us (17%)
  other arithmetic  314 us (16%)
  starting transfers between devices  82.6 us (4%)
  between operations  25 us (1%)
    psum x7, blocking collectives, global_dot(): lax.psum(jnp.sum(left_field * right_field / multiplicity), ('curve', 'spl...  692 us
    all_gather x4, waiting for transfers between devices, precondition(): lax.all_gather(partial_image, ('curve', 'split'), axis=0, tiled=False)  533 us
    scatter-add x5, other arithmetic, assemble(): jax.ops.segment_sum(values, point_slots, num_segments=node_count + 1)  218 us
    gather x5, local copies, waits for them, and re-layouts, assemble(): return assembled[:, point_slots].reshape(fields.shape)  210 us
    ppermute x30, starting transfers between devices, from_behind(): return lax.ppermute(block, axis, route)  82.4 us
    all_gather x4, local copies, waits for them, and re-layouts, precondition(): lax.all_gather(partial_image, ('curve', 'split'), axis=0, tiled=False)  72.9 us
  transfers between devices with their start and end apart: 34, of which 4 were waited for; matrix products, arithmetic and copies ran while one was open for 3% of the time, Pallas kernels for 0%

profile of v1, /device:TPU:27, one launch (start us, length us, event | category | flops | bytes accessed | tf_op | source)
XLA Modules:
  0.0 2008.3 jit_solution(11383894770662014076)
XLA Ops:
  14.6 2.6 copy.20
  17.2 45.0 %scatter_custom_fusion = f32[3,5489]{0,1:T(8,128)S(1)} fusion(s32[8192]{0:T(1024)S(1)} %bitcast.195, f32[8192,3]{1,0:T(8,128)} %copy.20, f32[]{:T(128)} %constant.10.clone.1), kind=kCustom, calls=%fused_computation.89 | custom fusion | flops 24576 | bytes 66380 | tf_op jit(solution)/shard_map/vmap()/scatter-add | solution.py:89
  62.9 4.4 collective-permute-start
  71.2 3.1 collective-permute-start.2
  75.5 3.9 collective-permute-start.3
  84.0 2.4 collective-permute-start.5
  86.6 2.3 scatter_custom_fusion.1
  88.9 2.4 scatter_custom_fusion.2
  91.3 2.3 scatter_custom_fusion.3
  93.6 2.3 scatter_custom_fusion.4
  95.9 2.3 scatter_custom_fusion.5
  98.2 2.7 scatter_custom_fusion.6
  100.9 27.7 %gather_fusion.6 = f32[8192,3]{1,0:T(8,128)} fusion(f32[3,5489]{0,1:T(8,128)S(1)} %scatter_custom_fusion.6, s32[8192]{0:T(1024)S(1)} %broadcast_clamp_fusion), kind=kCustom, calls=%fused_computation.6 | custom fusion | bytes 229376 | tf_op jit(solution)/shard_map/gather | solution.py:102
  128.6 10.2 slice_reduce_fusion.1
  140.6 2.9 scatter_custom_fusion.8
  143.8 140.8 %all-gather.9.cloned.1.call-done = f32[4194304]{0:T(1024)} async-done(((f32[8192]{0:T(1024)}), f32[4194304]{0:T(1024)}) %all-gather.9.cloned.1.call-update) | async-done | bytes 16777232 | tf_op jit(solution)/shard_map/all_gather | solution.py:183
  284.7 18.2 reshape.1193
  302.9 6.5 reduce_sum.144
  314.8 43.4 %scatter_custom_fusion.9 = f32[5489]{0:T(1024)S(1)} fusion(s32[8192]{0:T(1024)S(1)} %bitcast.196, f32[8192]{0:T(1024)S(1)} %bitcast.201, f32[]{:T(128)} %constant.10.clone.1), kind=kCustom, calls=%fused_computation.198 | custom fusion | flops 8192 | bytes 21960 | tf_op jit(solution)/shard_map/vmap()/scatter-add | solution.py:89
  363.0 3.4 collective-permute-start.6
  370.6 3.4 collective-permute-start.11
  375.9 4.0 collective-permute-start.9
  389.8 45.5 %gather_fusion.15 = f32[8192]{0:T(1024)S(1)} fusion(f32[5489]{0:T(1024)S(1)} %scatter_fusion.5, s32[8192]{0:T(1024)S(1)} %broadcast_clamp_fusion), kind=kCustom, calls=%fused_computation.15 | custom fusion | bytes 98304 | tf_op jit(solution)/shard_map/gather | solution.py:102
  436.1 99.8 %all-reduce = (f32[]{:T(128)}, f32[]{:T(128)}) all-reduce(f32[]{:T(128)} %get-tuple-element.6, f32[]{:T(128)} %get-tuple-element.5), channel_id=1, replica_groups=mesh['curve'=64,'split'=8] {'curve','split'}, use_global_device_ids=true, to_apply=%region_12.13 | all-reduce | flops 2 | bytes 16 | tf_op jit(solution)/shard_map/psum | solution.py:151
  539.1 3.0 scatter_custom_fusion.17
  542.3 130.6 %all-gather.11.cloned.1.call-done = f32[4194304]{0:T(1024)} async-done(((f32[8192]{0:T(1024)}), f32[4194304]{0:T(1024)}) %all-gather.11.cloned.1.call-update) | async-done | bytes 16777232 | tf_op jit(solution)/shard_map/all_gather | solution.py:183
  672.9 18.2 reshape.1194
  691.1 6.5 reduce_sum.148
  701.6 97.5 %psum.58 = f32[]{:T(128)} all-reduce(f32[]{:T(128)} %get-tuple-element.18), channel_id=1, replica_groups=mesh['curve'=64,'split'=8] {'curve','split'}, use_global_device_ids=true, to_apply=%region_27.28 | all-reduce | flops 1 | bytes 8 | tf_op jit(solution)/shard_map/psum | solution.py:151
  802.1 43.2 %scatter_custom_fusion.18 = f32[5489]{0:T(1024)S(1)} fusion(s32[8192]{0:T(1024)S(1)} %bitcast.197, f32[8192]{0:T(1024)S(1)} %bitcast.202, f32[]{:T(128)} %constant.10.clone.1), kind=kCustom, calls=%fused_computation.196 | custom fusion | flops 8192 | bytes 21960 | tf_op jit(solution)/shard_map/vmap()/scatter-add | solution.py:89
  850.5 3.2 collective-permute-start.12
  856.1 2.1 collective-permute-start.13
  860.1 3.4 collective-permute-start.14
  863.5 2.9 collective-permute-start.15
  866.4 2.3 collective-permute-start.16
  876.7 45.5 %gather_fusion.24 = f32[8192]{0:T(1024)S(1)} fusion(f32[5489]{0:T(1024)S(1)} %scatter_fusion.11, s32[8192]{0:T(1024)S(1)} %broadcast_clamp_fusion), kind=kCustom, calls=%fused_computation.24 | custom fusion | bytes 98304 | tf_op jit(solution)/shard_map/gather | solution.py:102
  922.8 100.2 %psum.59 = f32[]{:T(128)} all-reduce(f32[]{:T(128)} %fusion.33), channel_id=1, replica_groups=mesh['curve'=64,'split'=8] {'curve','split'}, use_global_device_ids=true, to_apply=%region_36.37 | all-reduce | flops 1 | bytes 8 | tf_op jit(solution)/shard_map/psum | solution.py:151
  1025.3 2.0 scatter_custom_fusion.25
  1027.4 3.0 scatter_custom_fusion.26
  1030.5 130.6 %all-gather.13.cloned.1.call-done = f32[4194304]{0:T(1024)} async-done(((f32[8192]{0:T(1024)}), f32[4194304]{0:T(1024)}) %all-gather.13.cloned.1.call-update) | async-done | bytes 16777232 | tf_op jit(solution)/shard_map/all_gather | solution.py:183
  1161.1 18.2 reshape.1195
  1179.3 6.5 reduce_sum.152
  1189.9 97.3 %psum.60 = f32[]{:T(128)} all-reduce(f32[]{:T(128)} %get-tuple-element.20), channel_id=1, replica_groups=mesh['curve'=64,'split'=8] {'curve','split'}, use_global_device_ids=true, to_apply=%region_42.43 | all-reduce | flops 1 | bytes 8 | tf_op jit(solution)/shard_map/psum | solution.py:151
  1290.2 43.2 %scatter_custom_fusion.27 = f32[5489]{0:T(1024)S(1)} fusion(s32[8192]{0:T(1024)S(1)} %bitcast.198, f32[8192]{0:T(1024)S(1)} %bitcast.203, f32[]{:T(128)} %constant.10.clone.1), kind=kCustom, calls=%fused_computation.194 | custom fusion | flops 8192 | bytes 21960 | tf_op jit(solution)/shard_map/vmap()/scatter-add | solution.py:89
  1338.6 3.2 collective-permute-start.18
  1344.3 2.1 collective-permute-start.19
  1348.3 3.4 collective-permute-start.20
  1351.7 2.9 collective-permute-start.21
  1354.6 2.3 collective-permute-start.22
  1365.1 45.5 %gather_fusion.33 = f32[8192]{0:T(1024)S(1)} fusion(f32[5489]{0:T(1024)S(1)} %scatter_fusion.17, s32[8192]{0:T(1024)S(1)} %broadcast_clamp_fusion), kind=kCustom, calls=%fused_computation.33 | custom fusion | bytes 98304 | tf_op jit(solution)/shard_map/gather | solution.py:102
  1411.2 100.2 %psum.61 = f32[]{:T(128)} all-reduce(f32[]{:T(128)} %fusion.35), channel_id=1, replica_groups=mesh['curve'=64,'split'=8] {'curve','split'}, use_global_device_ids=true, to_apply=%region_51.52 | all-reduce | flops 1 | bytes 8 | tf_op jit(solution)/shard_map/psum | solution.py:151
  1514.7 3.0 scatter_custom_fusion.35
  1517.7 130.7 %all-gather.15.cloned.1.call-done = f32[4194304]{0:T(1024)} async-done(((f32[8192]{0:T(1024)}), f32[4194304]{0:T(1024)}) %all-gather.15.cloned.1.call-update) | async-done | bytes 16777232 | tf_op jit(solution)/shard_map/all_gather | solution.py:183
  1648.4 18.2 reshape.1196
  1666.6 6.5 reduce_sum.156
  1677.2 97.3 %psum.62 = f32[]{:T(128)} all-reduce(f32[]{:T(128)} %get-tuple-element.22), channel_id=1, replica_groups=mesh['curve'=64,'split'=8] {'curve','split'}, use_global_device_ids=true, to_apply=%region_57.58 | all-reduce | flops 1 | bytes 8 | tf_op jit(solution)/shard_map/psum | solution.py:151
  1777.6 43.2 %scatter_custom_fusion.36 = f32[5489]{0:T(1024)S(1)} fusion(s32[8192]{0:T(1024)S(1)} %bitcast.199, f32[8192]{0:T(1024)S(1)} %bitcast.200, f32[]{:T(128)} %constant.10.clone.1), kind=kCustom, calls=%fused_computation.192 | custom fusion | flops 8192 | bytes 21960 | tf_op jit(solution)/shard_map/vmap()/scatter-add | solution.py:89
  1825.9 3.4 collective-permute-start.24
  1831.9 2.1 collective-permute-start.25
  1834.0 2.7 collective-permute-start.28
  1838.6 2.9 collective-permute-start.27
  1841.6 3.6 collective-permute-start.29
  1853.1 45.5 %gather_fusion.42 = f32[8192]{0:T(1024)S(1)} fusion(f32[5489]{0:T(1024)S(1)} %scatter_fusion.23, s32[8192]{0:T(1024)S(1)} %broadcast_clamp_fusion), kind=kCustom, calls=%fused_computation.42 | custom fusion | bytes 98304 | tf_op jit(solution)/shard_map/gather | solution.py:102
  1899.2 99.8 %psum.63 = f32[]{:T(128)} all-reduce(f32[]{:T(128)} %fusion.37), channel_id=1, replica_groups=mesh['curve'=64,'split'=8] {'curve','split'}, use_global_device_ids=true, to_apply=%region_66.67 | all-reduce | flops 1 | bytes 8 | tf_op jit(solution)/shard_map/psum | solution.py:151
  (281 shorter events, 123.6 us)
Async XLA Ops:
  7.2 277.5 %all-gather.9.cloned.1.call-start = ((), (), s32[]{:S(2)}) async-start(), calls=%async_computation | async-start | bytes 16809984 | tf_op jit(solution)/shard_map/all_gather | solution.py:183
  8.8 1281.3 %copy-start.13 = (f32[16]{0:T(128)}, f32[16]{0:T(128)S(1)}, u32[]{:S(2)}) copy-start(f32[16]{0:T(128)S(1)} %get-tuple-element.13) | copy-start | bytes 196
  8.8 1281.3 %copy-start.15 = (f32[16]{0:T(128)}, f32[16]{0:T(128)S(1)}, u32[]{:S(2)}) copy-start(f32[16]{0:T(128)S(1)} %get-tuple-element.14) | copy-start | bytes 196
  8.8 1281.3 %copy-start.17 = (f32[16]{0:T(128)}, f32[16]{0:T(128)S(1)}, u32[]{:S(2)}) copy-start(f32[16]{0:T(128)S(1)} %get-tuple-element.15) | copy-start | bytes 196
  14.5 55.3 %copy-start.32 = (s32[1,1,4,128]{3,2,1,0:T(4,128)S(1)}, s32[1,1,4,128]{3,2,1,0:T(4,128)}, u32[]{:S(2)}) copy-start(s32[1,1,4,128]{3,2,1,0:T(4,128)} %param.18) | copy-start | bytes 6148
  14.5 68.1 %copy-start.2 = (s32[16,512]{1,0:T(8,128)S(1)}, s32[16,512]{1,0:T(8,128)}, u32[]{:S(2)}) copy-start(s32[16,512]{1,0:T(8,128)} %param.17) | copy-start | bytes 98308
  14.5 71.9 %copy-start.19 = (s32[8,16]{1,0:T(8,128)S(1)}, s32[8,16]{1,0:T(8,128)}, u32[]{:S(2)}) copy-start(s32[8,16]{1,0:T(8,128)} %param.20) | copy-start | bytes 1540
  14.6 72.0 %copy-start.5 = (s32[16,16]{1,0:T(8,128)S(1)}, s32[16,16]{1,0:T(8,128)}, u32[]{:S(2)}) copy-start(s32[16,16]{1,0:T(8,128)} %param.22) | copy-start | bytes 3076
  17.2 344.6 %copy-start.27 = (s32[1024]{0:T(1024)}, s32[1024]{0:T(1024)S(1)}, u32[]{:S(2)}) copy-start(s32[1024]{0:T(1024)S(1)} %get-tuple-element.27) | copy-start | bytes 12292
  17.2 836.5 %copy-start.26 = (s32[1024]{0:T(1024)}, s32[1024]{0:T(1024)S(1)}, u32[]{:S(2)}) copy-start(s32[1024]{0:T(1024)S(1)} %get-tuple-element.26) | copy-start | bytes 12292
  62.9 21.1 %collective-permute-start = (f32[3,128]{0,1:T(8,128)S(1)}, f32[3,128]{0,1:T(8,128)S(1)}, u32[]{:S(2)}, u32[]{:S(2)}) collective-permute-start(f32[3,128]{0,1:T(8,128)S(1)} %bitcast.253), channel_id=1, source_target_pairs={{0,1},{1,2},{2,3},{3,4},{4,5},{5,6},{6,7},{8,9},{9,10},{10,11},{11... | collective-permute-start | bytes 4616 | tf_op jit(solution)/shard_map/ppermute | solution.py:13
  67.9 21.0 %collective-permute-start.1 = (f32[3,128]{0,1:T(8,128)S(1)}, f32[3,128]{0,1:T(8,128)S(1)}, u32[]{:S(2)}, u32[]{:S(2)}) collective-permute-start(f32[3,128]{0,1:T(8,128)S(1)} %bitcast.252), channel_id=1, source_target_pairs={{1,0},{2,1},{3,2},{4,3},{5,4},{6,5},{7,6},{9,8},{10,9},{11,10},{12... | collective-permute-start | bytes 4616 | tf_op jit(solution)/shard_map/ppermute | solution.py:13
  69.9 801.5 %copy-start.10 = (s32[128]{0:T(128)}, s32[128]{0:T(128)S(1)}, u32[]{:S(2)}) copy-start(s32[128]{0:T(128)S(1)} %get-tuple-element.11) | copy-start | bytes 1540
  69.9 802.8 %copy-start.8 = (s32[128]{0:T(128)}, s32[128]{0:T(128)S(1)}, u32[]{:S(2)}) copy-start(s32[128]{0:T(128)S(1)} %get-tuple-element.12) | copy-start | bytes 1540
  69.9 804.2 %copy-start.6 = (s32[128]{0:T(128)}, s32[128]{0:T(128)S(1)}, u32[]{:S(2)}) copy-start(s32[128]{0:T(128)S(1)} %get-tuple-element.9) | copy-start | bytes 1540
  69.9 289.5 %copy-start.29 = (s32[1024]{0:T(1024)}, s32[1024]{0:T(1024)S(1)}, u32[]{:S(2)}) copy-start(s32[1024]{0:T(1024)S(1)} %get-tuple-element.30) | copy-start | bytes 12292
  69.9 290.7 %copy-start.28 = (s32[1024]{0:T(1024)}, s32[1024]{0:T(1024)S(1)}, u32[]{:S(2)}) copy-start(s32[1024]{0:T(1024)S(1)} %get-tuple-element.31) | copy-start | bytes 12292
  71.2 20.1 %collective-permute-start.2 = (f32[3,128]{0,1:T(8,128)}, f32[3,128]{0,1:T(8,128)S(1)}, u32[]{:S(2)}, u32[]{:S(2)}) collective-permute-start(f32[3,128]{0,1:T(8,128)} %bitcast.16), channel_id=1, source_target_pairs={{0,16},{8,24},{16,32},{24,40},{32,48},{40,56},{48,64},{56,72},{64,... | collective-permute-start | bytes 4616 | tf_op jit(solution)/shard_map/ppermute | solution.py:13
  75.5 18.1 collective-permute-start.3
  79.5 11.8 copy-start.31
  79.5 288.0 %copy-start.30 = (s32[1024]{0:T(1024)}, s32[1024]{0:T(1024)S(1)}, u32[]{:S(2)}) copy-start(s32[1024]{0:T(1024)S(1)} %get-tuple-element.28) | copy-start | bytes 12292
  80.7 15.1 collective-permute-start.4
  84.0 14.2 collective-permute-start.5
  86.5 52.5 %copy-start.34 = (s32[128]{0:T(128)}, s32[128]{0:T(128)S(1)}, u32[]{:S(2)}) copy-start(s32[128]{0:T(128)S(1)} %reshape.851) | copy-start | bytes 1540
  86.6 54.0 %copy-start.33 = (s32[256]{0:T(256)}, s32[256]{0:T(256)S(1)}, u32[]{:S(2)}) copy-start(s32[256]{0:T(256)S(1)} %reshape.859) | copy-start | bytes 3076
  128.6 10.2 copy-start.20
  128.6 11.9 copy-start.1
  128.6 11.9 copy-start.4
  143.6 529.3 %all-gather.11.cloned.1.call-start = ((), (), s32[]{:S(2)}) async-start(), calls=%async_computation.1 | async-start | bytes 16809984 | tf_op jit(solution)/shard_map/all_gather | solution.py:183
  363.0 17.0 collective-permute-start.6
  368.7 14.5 collective-permute-start.7
  370.6 17.9 collective-permute-start.11
  374.0 10.6 collective-permute-start.8
  375.9 9.9 collective-permute-start.9
  380.0 7.2 collective-permute-start.10
  542.2 618.9 %all-gather.13.cloned.1.call-start = ((), (), s32[]{:S(2)}) async-start(), calls=%async_computation.2 | async-start | bytes 16809984 | tf_op jit(solution)/shard_map/all_gather | solution.py:183
  850.5 15.9 collective-permute-start.12
  856.1 13.9 collective-permute-start.13
  858.2 17.2 collective-permute-start.17
  860.1 11.3 collective-permute-start.14
  863.5 9.2 collective-permute-start.15
  866.4 7.6 collective-permute-start.16
  1030.4 618.0 %all-gather.15.cloned.1.call-start = ((), (), s32[]{:S(2)}) async-start(), calls=%async_computation.3 | async-start | bytes 16809984 | tf_op jit(solution)/shard_map/all_gather | solution.py:183
  1290.1 69.5 %copy-start.11 = (s32[128]{0:T(128)S(1)}, s32[128]{0:T(128)}, u32[]{:S(2)}) copy-start(s32[128]{0:T(128)} %copy-done.10) | copy-start | bytes 1540
  1334.7 26.2 %copy-start.9 = (s32[128]{0:T(128)S(1)}, s32[128]{0:T(128)}, u32[]{:S(2)}) copy-start(s32[128]{0:T(128)} %copy-done.8) | copy-start | bytes 1540
  1337.3 25.0 %copy-start.7 = (s32[128]{0:T(128)S(1)}, s32[128]{0:T(128)}, u32[]{:S(2)}) copy-start(s32[128]{0:T(128)} %copy-done.6) | copy-start | bytes 1540
  1338.6 16.1 collective-permute-start.18
  1344.3 13.9 collective-permute-start.19
  1346.4 17.3 collective-permute-start.23
  1348.3 11.3 collective-permute-start.20
  1351.7 9.2 collective-permute-start.21
  1354.6 7.6 collective-permute-start.22
  1365.1 147.7 %copy-start.22 = (f32[8,512]{1,0:T(8,128)S(1)}, f32[8,512]{1,0:T(8,128)}, u32[]{:S(2)}) copy-start(f32[8,512]{1,0:T(8,128)} %constant.4.clone) | copy-start | bytes 49156
  1676.3 101.2 %copy-start.14 = (f32[16]{0:T(128)S(1)}, f32[16]{0:T(128)}, u32[]{:S(2)}) copy-start(f32[16]{0:T(128)} %copy-done.13) | copy-start | bytes 196
  1676.3 101.2 %copy-start.16 = (f32[16]{0:T(128)S(1)}, f32[16]{0:T(128)}, u32[]{:S(2)}) copy-start(f32[16]{0:T(128)} %copy-done.15) | copy-start | bytes 196
  1676.3 101.1 %copy-start.18 = (f32[16]{0:T(128)S(1)}, f32[16]{0:T(128)}, u32[]{:S(2)}) copy-start(f32[16]{0:T(128)} %copy-done.17) | copy-start | bytes 196
  1676.3 101.1 %copy-start.25 = (f32[16]{0:T(128)S(1)}, f32[16]{0:T(128)}, u32[]{:S(2)}) copy-start(f32[16]{0:T(128)} %param.16) | copy-start | bytes 196
  1777.5 70.4 %copy-start.12 = (s32[128]{0:T(128)S(1)}, s32[128]{0:T(128)}, u32[]{:S(2)}) copy-start(s32[128]{0:T(128)} %copy-done.10) | copy-start | bytes 1540
  1825.9 15.7 collective-permute-start.24
  1831.9 14.5 collective-permute-start.25
  1834.0 16.5 collective-permute-start.28
  1836.7 11.1 collective-permute-start.26
  1838.6 10.5 collective-permute-start.27
  1841.6 10.2 collective-permute-start.29
  (5 other events, 11.5 us)
Sparse Core Ops, SparseCore 0:
  143.7 140.9 all-gather.8
  542.3 130.4 all-gather.10
  1030.6 130.5 all-gather.12
  1517.9 130.5 all-gather.14
